TPU v7x, 32 devices: a whole 2x2x4 slice. The times are simulated.
32 devices in a mesh: step: 8 (over y, x, core), lat: 4 (over z).
Axes of the slice: x: 2, y: 2, z: 4, core: 2. Of those that a mesh axis runs over, the one named last changes fastest.
Arguments:
- state_in: bfloat16 [8, 72, 64, 128], P('step', None, 'lat'), may hold values from -6 to 6
- new_state: bfloat16 [72, 64, 128], P(None, 'lat'), may hold values from -6 to 6
- cot_early: bfloat16 [8, 72, 64, 128], P('step', None, 'lat'), may hold values from -6 to 6
- cot_late: bfloat16 [8, 72, 64, 128], P('step', None, 'lat'), may hold values from -6 to 6
- kernel_first: bfloat16 [9, 72, 192], replicated, may hold values from -0.25 to 0.25
- kernel_mid: bfloat16 [9, 192, 192], replicated, may hold values from -0.15625 to 0.15625
- kernel_last: bfloat16 [9, 72, 192], replicated, may hold values from -0.15625 to 0.15625
Outputs:
- advanced: bfloat16 [8, 72, 64, 128], P('step', None, 'lat')
- state_adjoint: bfloat16 [8, 72, 64, 128], P('step', None, 'lat')
- grad_first: float32 [9, 72, 192], replicated
- grad_mid: float32 [9, 192, 192], replicated
- grad_last: float32 [9, 72, 192], replicated
All inputs are finite; a program needn't handle non-finite values.
Results may differ from a plain program's by a relative error of at most 0.008.
Values may be sent and summed in bfloat16 or wider, within the bound.
A program may use at most 64 MiB of HBM per device.

v0:
```python
import math
import jax
import jax.numpy as jnp
from jax import lax
from jax.sharding import PartitionSpec as P


def padded_2(block, sides, width):
    for axis, dim in sides:
        count = lax.axis_size(axis)
        forward = [(i, i + 1) for i in range(count - 1)]
        backward = [(target, source) for source, target in forward]
        low = lax.ppermute(
            lax.slice_in_dim(block, block.shape[dim] - width, None, axis=dim), axis, forward
        )
        high = lax.ppermute(lax.slice_in_dim(block, 0, width, axis=dim), axis, backward)
        block = jnp.concatenate([low, block, high], axis=dim)
    return block


def shifted(block, axis, distance):
    devices = range(lax.axis_size(axis))
    route = [(i - distance, i) for i in devices if i - distance in devices]
    return lax.ppermute(block, axis, route)


def window_at(padded, dilation, row_tap, col_tap, out_rows, out_cols):
    widened = jnp.pad(padded, ((0, 0), (0, 0), (dilation, dilation)))
    return widened[
        :,
        row_tap * dilation : row_tap * dilation + out_rows,
        col_tap * dilation : col_tap * dilation + out_cols,
    ]


def convolve(padded, kernel, dilation, flipped):
    out_rows = padded.shape[1] - 2 * dilation
    out_cols = padded.shape[2]
    pattern = "oc,crw->orw" if flipped else "co,crw->orw"
    summed = None
    for tap_index in range(9):
        window = window_at(padded, dilation, tap_index // 3, tap_index % 3, out_rows, out_cols)
        product = jnp.einsum(pattern, kernel[tap_index], window, preferred_element_type=jnp.float32)
        summed = product if summed is None else summed + product
    return summed


def convolve_back(padded, kernel, dilation, flipped):
    out_rows = padded.shape[1] - 2 * dilation
    out_cols = padded.shape[2]
    pattern = "oc,orw->crw" if flipped else "co,orw->crw"
    summed = None
    for tap_index in range(9):
        window = window_at(
            padded, dilation, 2 - tap_index // 3, 2 - tap_index % 3, out_rows, out_cols
        )
        product = jnp.einsum(pattern, kernel[tap_index], window, preferred_element_type=jnp.float32)
        summed = product if summed is None else summed + product
    return summed


def kernel_terms(padded_in, grad_out, dilation, flipped):
    out_rows = grad_out.shape[1]
    out_cols = grad_out.shape[2]
    pattern = "crw,orw->oc" if flipped else "crw,orw->co"
    listed = []
    for tap_index in range(9):
        window = window_at(padded_in, dilation, tap_index // 3, tap_index % 3, out_rows, out_cols)
        listed.append(jnp.einsum(pattern, window, grad_out, preferred_element_type=jnp.float32))
    return jnp.stack(listed)


def gelu_slope(preact, cotangent):
    return jax.vjp(jax.nn.gelu, preact)[1](cotangent)[0]


def body(state_in, new_state, cot_early, cot_late, kernel_first, kernel_mid, kernel_last):
    band_rows = state_in.shape[2]
    total_rows = band_rows * lax.axis_size("lat")
    band_index = lax.axis_index("lat")

    def inside(values, margin):
        local_rows = jnp.arange(values.shape[1], dtype=jnp.int32)
        global_row = band_index * band_rows + local_rows - margin
        keep = (global_row >= 0) & (global_row < total_rows)
        return jnp.where(keep[None, :, None], values, jnp.zeros_like(values))

    def advance(state):
        extended = padded_2(state, (("lat", 1),), 7)
        pre_first = convolve(extended, kernel_first, 1, False)
        hid_first = inside(jax.nn.gelu(pre_first).astype(jnp.bfloat16), 6)
        pre_mid = convolve(hid_first, kernel_mid, 2, False)
        hid_mid = inside(jax.nn.gelu(pre_mid).astype(jnp.bfloat16), 4)
        pre_last = convolve(hid_mid, kernel_last, 4, True)
        saved = (
            extended[:, 6 : 6 + band_rows + 2],
            hid_first[:, 4 : 4 + band_rows + 4],
            hid_mid,
            pre_first[:, 6 : 6 + band_rows],
            pre_mid[:, 4 : 4 + band_rows],
        )
        output = (state.astype(jnp.float32) + pre_last).astype(jnp.bfloat16)
        return (output, saved)

    def backward(cot_out, saved):
        in_first, in_mid, in_last, pre_first, pre_mid = saved
        pad_last = padded_2(cot_out, (("lat", 1),), 4)
        back_mid = convolve_back(pad_last, kernel_last, 4, True)
        grads_last = kernel_terms(in_last, cot_out, 4, True)
        delta_mid = gelu_slope(pre_mid, back_mid).astype(jnp.bfloat16)
        pad_mid = padded_2(delta_mid, (("lat", 1),), 2)
        back_first = convolve_back(pad_mid, kernel_mid, 2, False)
        grads_mid = kernel_terms(in_mid, delta_mid, 2, False)
        delta_first = gelu_slope(pre_first, back_first).astype(jnp.bfloat16)
        pad_first = padded_2(delta_first, (("lat", 1),), 1)
        back_state = convolve_back(pad_first, kernel_first, 1, False)
        grads_first = kernel_terms(in_first, delta_first, 1, False)
        adjoint = (cot_out.astype(jnp.float32) + back_state).astype(jnp.bfloat16)
        return (adjoint, (grads_first, grads_mid, grads_last))

    early_out, early_saved = advance(state_in[0])
    passed = shifted(early_out, "step", 1)
    late_in = jnp.where(lax.axis_index("step") == 0, new_state, passed)
    late_out, late_saved = advance(late_in)
    late_adjoint, late_grads = backward(cot_late[0], late_saved)
    returned = shifted(late_adjoint, "step", -1)
    early_cot = (cot_early[0].astype(jnp.float32) + returned.astype(jnp.float32)).astype(
        jnp.bfloat16
    )
    state_adjoint, early_grads = backward(early_cot, early_saved)
    grand_total = lax.psum(
        (
            late_grads[0] + early_grads[0],
            late_grads[1] + early_grads[1],
            late_grads[2] + early_grads[2],
        ),
        ("step", "lat"),
    )
    cell_count = 2.0 * lax.axis_size("step") * total_rows * state_in.shape[3]
    grad_scale = 1.0 / math.sqrt(cell_count)
    return (
        late_out[None],
        state_adjoint[None],
        grand_total[0] * grad_scale,
        grand_total[1] * grad_scale,
        grand_total[2] * grad_scale,
    )


def solution(mesh):
    in_specs = (
        P("step", None, "lat", None),
        P(None, "lat", None),
        P("step", None, "lat", None),
        P("step", None, "lat", None),
        P(),
        P(),
        P(),
    )
    out_specs = (P("step", None, "lat", None), P("step", None, "lat", None), P(), P(), P())
    return jax.shard_map(body, mesh=mesh, in_specs=in_specs, out_specs=out_specs, check_vma=False)
```

profile of v0, /device:TPU:0, one launch (start us, length us, event | category | flops | bytes accessed | tf_op | source)
XLA Modules:
  0.0 348.6 jit_solution(4227039910495838793)
XLA Ops:
  8.4 5.0 %collective-permute-start = (bf16[72,7,128]{2,0,1:T(8,128)(2,1)S(1)}, bf16[72,7,128]{2,0,1:T(8,128)(2,1)S(1)}, u32[]{:S(2)}, u32[]{:S(2)}) collective-permute-start(bf16[72,7,128]{2,0,1:T(8,128)(2,1)S(1)} %get-tuple-element.27), channel_id=1, source_target_pairs={{0,1},{1,2},{2,3},{4,5},{5,6},{6,7},{8,9},{9,10},{10,11},{12,13},{... | collective-permute-start | bytes 387080 | tf_op jit(solution)/shard_map/ppermute | solution.py:13
  15.7 4.5 %collective-permute-start.5 = (bf16[72,4,128]{2,0,1:T(8,128)(2,1)S(1)}, bf16[72,4,128]{2,0,1:T(8,128)(2,1)S(1)}, u32[]{:S(2)}, u32[]{:S(2)}) collective-permute-start(bf16[72,4,128]{2,0,1:T(8,128)(2,1)S(1)} %get-tuple-element.24), channel_id=1, source_target_pairs={{0,1},{1,2},{2,3},{4,5},{5,6},{6,7},{8,9},{9,10},{10,11},{12,13},{... | collective-permute-start | bytes 221192 | tf_op jit(solution)/shard_map/ppermute | solution.py:13
  21.6 1.6 fusion.442
  23.2 3.3 collective-permute-done.6
  26.9 1.7 fusion.338
  30.2 1.6 fusion.342
  38.3 3.8 %fusion.75 = (bf16[192,28,128]{2,0,1:T(8,128)(2,1)S(1)}, f32[192,28,128]{2,0,1:T(8,128)}) fusion(pred[28]{0:T(512)(128)(4,1)S(1)} %compare_and_fusion, bf16[9,72,192]{2,1,0:T(8,128)(2,1)S(1)} %copy-done.8, bf16[72,30,128]{2,0,1:T(8,128)(2,1)S(1)} %pad_maximum_fusion, f32[28,128,192]{1,2,0:T(8,128)S(1)} %fusion.470, f32[28,128,192]{1,2,0:T(8,128)S(1)} %fusion.273, ...), kind=kOutput, calls=%fused_computation.167 | convolution fusion | flops 111476736 | bytes 26739200 | tf_op jit(solution)/shard_map/co,crw->orw/dot_general | solution.py:43
  46.5 3.3 fusion.129
  57.0 1.6 fusion.346
  58.7 3.5 collective-permute-start.3
  66.1 2.9 collective-permute-done.4
  74.7 12.8 %fusion.74 = (bf16[192,28,128]{2,0,1:T(8,128)(2,1)S(1)}, f32[192,28,128]{2,0,1:T(8,128)}) fusion(pred[28]{0:T(512)(128)(4,1)S(1)} %compare_and_fusion, bf16[9,72,192]{2,1,0:T(8,128)(2,1)} %param.11, bf16[72,30,128]{2,0,1:T(8,128)(2,1)S(1)} %pad_maximum_fusion.1, f32[28,128,192]{1,2,0:T(8,128)S(1)} %fusion.468, f32[28,128,192]{1,2,0:T(8,128)S(1)} %fusion.279, ...), kind=kOutput, calls=%fused_computation.166 | convolution fusion | flops 111476736 | bytes 26738716 | tf_op jit(solution)/shard_map/co,crw->orw/dot_general | solution.py:43
  92.0 2.0 fusion.128
  94.0 6.1 %fusion.43 = bf16[192,16,128]{2,0,1:T(8,128)(2,1)S(1)} fusion(f32[16,128,192]{1,2,0:T(8,128)} %fusion.309, f32[16,128,192]{1,2,0:T(8,128)} %fusion.338, f32[16,128,192]{1,2,0:T(8,128)} %fusion.340, f32[192,16,128]{2,0,1:T(8,128)S(1)} %copy-done.6, f32[192,24,128]{2,0,1:T(8,128)S(1)} %get-tuple-element.36, f32[16,128,192]{1,2,0:T(8,128)} %fusion.342, ...), kind=kOutput, calls=%fused_computation.121 | convolution fusion | flops 67633152 | bytes 15273984 | tf_op jit(solution)/shard_map/oc,orw->crw/dot_general | solution.py:57
  104.9 4.8 %collective-permute-start.7 = (bf16[192,2,128]{2,0,1:T(8,128)(2,1)S(1)}, bf16[192,2,128]{2,0,1:T(8,128)(2,1)S(1)}, u32[]{:S(2)}, u32[]{:S(2)}) collective-permute-start(bf16[192,2,128]{2,0,1:T(8,128)(2,1)S(1)} %get-tuple-element.20), channel_id=1, source_target_pairs={{0,1},{1,2},{2,3},{4,5},{5,6},{6,7},{8,9},{9,10},{10,11},{12,13},{... | collective-permute-start | bytes 294920 | tf_op jit(solution)/shard_map/ppermute | solution.py:13
  123.8 1.7 fusion.50
  127.1 5.0 %collective-permute-start.9 = (bf16[192,1,128]{2,0,1:T(8,128)(2,1)S(1)}, bf16[192,1,128]{2,0,1:T(8,128)(2,1)S(1)}, u32[]{:S(2)}, u32[]{:S(2)}) collective-permute-start(bf16[192,1,128]{2,0,1:T(8,128)(2,1)S(1)} %get-tuple-element.17), channel_id=1, source_target_pairs={{0,1},{1,2},{2,3},{4,5},{5,6},{6,7},{8,9},{9,10},{10,11},{12,13},{... | collective-permute-start | bytes 147464 | tf_op jit(solution)/shard_map/ppermute | solution.py:13
  147.4 4.7 %collective-permute-start.12 = (bf16[72,4,128]{2,0,1:T(8,128)(2,1)S(1)}, bf16[72,4,128]{2,0,1:T(8,128)(2,1)S(1)}, u32[]{:S(2)}, u32[]{:S(2)}) collective-permute-start(bf16[72,4,128]{2,0,1:T(8,128)(2,1)S(1)} %get-tuple-element.22), channel_id=1, source_target_pairs={{0,1},{1,2},{2,3},{4,5},{5,6},{6,7},{8,9},{9,10},{10,11},{12,13},{... | collective-permute-start | bytes 221192 | tf_op jit(solution)/shard_map/ppermute | solution.py:13
  158.3 1.7 fusion.57
  165.9 5.1 %collective-permute-start.14 = (bf16[192,2,128]{2,0,1:T(8,128)(2,1)S(1)}, bf16[192,2,128]{2,0,1:T(8,128)(2,1)S(1)}, u32[]{:S(2)}, u32[]{:S(2)}) collective-permute-start(bf16[192,2,128]{2,0,1:T(8,128)(2,1)S(1)} %get-tuple-element.16), channel_id=1, source_target_pairs={{0,1},{1,2},{2,3},{4,5},{5,6},{6,7},{8,9},{9,10},{10,11},{12,13},{... | collective-permute-start | bytes 294920 | tf_op jit(solution)/shard_map/ppermute | solution.py:13
  177.5 1.7 fusion.64
  183.8 5.2 %collective-permute-start.16 = (bf16[192,1,128]{2,0,1:T(8,128)(2,1)S(1)}, bf16[192,1,128]{2,0,1:T(8,128)(2,1)S(1)}, u32[]{:S(2)}, u32[]{:S(2)}) collective-permute-start(bf16[192,1,128]{2,0,1:T(8,128)(2,1)S(1)} %get-tuple-element.13), channel_id=1, source_target_pairs={{0,1},{1,2},{2,3},{4,5},{5,6},{6,7},{8,9},{9,10},{10,11},{12,13},{... | collective-permute-start | bytes 147464 | tf_op jit(solution)/shard_map/ppermute | solution.py:13
  195.3 142.1 %all-reduce.19.cloned.1.call-done = (f32[9,72,192]{2,1,0:T(8,128)}, f32[9,192,192]{2,1,0:T(8,128)}, f32[9,72,192]{2,1,0:T(8,128)}) async-done(((f32[9,72,192]{2,1,0:T(8,128)}, f32[9,192,192]{2,1,0:T(8,128)}, f32[9,72,192]{2,1,0:T(8,128)}), (f32[9,72,192]{2,1,0:T(8,128)}, f32[9,192,192]{2,1,0:T(8,128)}, f32[9,72,192]{2,1,0:T(8,128)})) %all-reduce.19.cloned.1.call-update) | async-done | bytes 2322448 | tf_op jit(solution)/shard_map/psum | solution.py:131
  337.4 2.9 broadcast_multiply_fusion
  (270 shorter events, 104.4 us)
Async XLA Ops:
  7.2 14.4 %copy-start = (bf16[1,72,16,128]{3,2,1,0:T(8,128)(2,1)S(1)}, bf16[1,72,16,128]{3,2,1,0:T(8,128)(2,1)}, u32[]{:S(2)}) copy-start(bf16[1,72,16,128]{3,2,1,0:T(8,128)(2,1)} %param.10) | copy-start | bytes 884740
  7.2 14.4 %copy-start.7 = (bf16[9,72,192]{2,1,0:T(8,128)(2,1)S(1)}, bf16[9,72,192]{2,1,0:T(8,128)(2,1)}, u32[]{:S(2)}) copy-start(bf16[9,72,192]{2,1,0:T(8,128)(2,1)} %param.13) | copy-start | bytes 746500
  7.2 330.2 %all-reduce.19.cloned.1.call-start = ((), (), s32[]{:S(2)}) async-start(), calls=%async_computation | async-start | bytes 6193152 | tf_op jit(solution)/shard_map/psum | solution.py:131
  8.4 25.0 %collective-permute-start = (bf16[72,7,128]{2,0,1:T(8,128)(2,1)S(1)}, bf16[72,7,128]{2,0,1:T(8,128)(2,1)S(1)}, u32[]{:S(2)}, u32[]{:S(2)}) collective-permute-start(bf16[72,7,128]{2,0,1:T(8,128)(2,1)S(1)} %get-tuple-element.27), channel_id=1, source_target_pairs={{0,1},{1,2},{2,3},{4,5},{5,6},{6,7},{8,9},{9,10},{10,11},{12,13},{... | collective-permute-start | bytes 387080 | tf_op jit(solution)/shard_map/ppermute | solution.py:13
  13.3 20.0 %collective-permute-start.1 = (bf16[72,7,128]{2,0,1:T(8,128)(2,1)S(1)}, bf16[72,7,128]{2,0,1:T(8,128)(2,1)S(1)}, u32[]{:S(2)}, u32[]{:S(2)}) collective-permute-start(bf16[72,7,128]{2,0,1:T(8,128)(2,1)S(1)} %get-tuple-element.28), channel_id=1, source_target_pairs={{1,0},{2,1},{3,2},{5,4},{6,5},{7,6},{9,8},{10,9},{11,10},{13,12},{... | collective-permute-start | bytes 387080 | tf_op jit(solution)/shard_map/ppermute | solution.py:16
  15.7 7.5 %collective-permute-start.5 = (bf16[72,4,128]{2,0,1:T(8,128)(2,1)S(1)}, bf16[72,4,128]{2,0,1:T(8,128)(2,1)S(1)}, u32[]{:S(2)}, u32[]{:S(2)}) collective-permute-start(bf16[72,4,128]{2,0,1:T(8,128)(2,1)S(1)} %get-tuple-element.24), channel_id=1, source_target_pairs={{0,1},{1,2},{2,3},{4,5},{5,6},{6,7},{8,9},{9,10},{10,11},{12,13},{... | collective-permute-start | bytes 221192 | tf_op jit(solution)/shard_map/ppermute | solution.py:13
  20.3 6.2 %collective-permute-start.6 = (bf16[72,4,128]{2,0,1:T(8,128)(2,1)S(1)}, bf16[72,4,128]{2,0,1:T(8,128)(2,1)S(1)}, u32[]{:S(2)}, u32[]{:S(2)}) collective-permute-start(bf16[72,4,128]{2,0,1:T(8,128)(2,1)S(1)} %get-tuple-element.23), channel_id=1, source_target_pairs={{1,0},{2,1},{3,2},{5,4},{6,5},{7,6},{9,8},{10,9},{11,10},{13,12},{... | collective-permute-start | bytes 221192 | tf_op jit(solution)/shard_map/ppermute | solution.py:16
  26.9 30.1 %copy-start.2 = (bf16[72,24,136]{2,0,1:T(8,128)(2,1)}, bf16[72,24,136]{2,0,1:T(8,128)(2,1)S(1)}, u32[]{:S(2)}) copy-start(bf16[72,24,136]{2,0,1:T(8,128)(2,1)S(1)} %select_maximum_fusion.10) | copy-start | bytes 1410052
  54.0 4.6 %collective-permute-start.2 = (bf16[72,16,128]{2,0,1:T(8,128)(2,1)S(1)}, bf16[72,16,128]{2,0,1:T(8,128)(2,1)S(1)}, u32[]{:S(2)}, u32[]{:S(2)}) collective-permute-start(bf16[72,16,128]{2,0,1:T(8,128)(2,1)S(1)} %fusion.105), channel_id=1, source_target_pairs={{0,4},{4,8},{8,12},{12,16},{16,20},{20,24},{24,28},{1,5},{5,9},{9,... | collective-permute-start | bytes 884744 | tf_op jit(solution)/shard_map/ppermute | solution.py:24
  58.7 7.4 %collective-permute-start.3 = (bf16[72,7,128]{2,0,1:T(8,128)(2,1)S(1)}, bf16[72,7,128]{2,0,1:T(8,128)(2,1)S(1)}, u32[]{:S(2)}, u32[]{:S(2)}) collective-permute-start(bf16[72,7,128]{2,0,1:T(8,128)(2,1)S(1)} %get-tuple-element.25), channel_id=1, source_target_pairs={{0,1},{1,2},{2,3},{4,5},{5,6},{6,7},{8,9},{9,10},{10,11},{12,13},{... | collective-permute-start | bytes 387080 | tf_op jit(solution)/shard_map/ppermute | solution.py:13
  62.2 6.8 %collective-permute-start.4 = (bf16[72,7,128]{2,0,1:T(8,128)(2,1)S(1)}, bf16[72,7,128]{2,0,1:T(8,128)(2,1)S(1)}, u32[]{:S(2)}, u32[]{:S(2)}) collective-permute-start(bf16[72,7,128]{2,0,1:T(8,128)(2,1)S(1)} %get-tuple-element.26), channel_id=1, source_target_pairs={{1,0},{2,1},{3,2},{5,4},{6,5},{7,6},{9,8},{10,9},{11,10},{13,12},{... | collective-permute-start | bytes 387080 | tf_op jit(solution)/shard_map/ppermute | solution.py:16
  66.1 7.3 %copy-start.19 = (bf16[72,7,128]{2,0,1:T(8,128)(2,1)}, bf16[72,7,128]{2,0,1:T(8,128)(2,1)S(1)}, u32[]{:S(2)}) copy-start(bf16[72,7,128]{2,0,1:T(8,128)(2,1)S(1)} %collective-permute-done.3) | copy-start | bytes 387076
  103.6 15.1 %collective-permute-start.8 = (bf16[192,2,128]{2,0,1:T(8,128)(2,1)S(1)}, bf16[192,2,128]{2,0,1:T(8,128)(2,1)S(1)}, u32[]{:S(2)}, u32[]{:S(2)}) collective-permute-start(bf16[192,2,128]{2,0,1:T(8,128)(2,1)S(1)} %get-tuple-element.19), channel_id=1, source_target_pairs={{1,0},{2,1},{3,2},{5,4},{6,5},{7,6},{9,8},{10,9},{11,10},{13,12},{... | collective-permute-start | bytes 294920 | tf_op jit(solution)/shard_map/ppermute | solution.py:16
  104.9 13.8 %collective-permute-start.7 = (bf16[192,2,128]{2,0,1:T(8,128)(2,1)S(1)}, bf16[192,2,128]{2,0,1:T(8,128)(2,1)S(1)}, u32[]{:S(2)}, u32[]{:S(2)}) collective-permute-start(bf16[192,2,128]{2,0,1:T(8,128)(2,1)S(1)} %get-tuple-element.20), channel_id=1, source_target_pairs={{0,1},{1,2},{2,3},{4,5},{5,6},{6,7},{8,9},{9,10},{10,11},{12,13},{... | collective-permute-start | bytes 294920 | tf_op jit(solution)/shard_map/ppermute | solution.py:13
  125.8 9.1 %collective-permute-start.10 = (bf16[192,1,128]{2,0,1:T(8,128)(2,1)S(1)}, bf16[192,1,128]{2,0,1:T(8,128)(2,1)S(1)}, u32[]{:S(2)}, u32[]{:S(2)}) collective-permute-start(bf16[192,1,128]{2,0,1:T(8,128)(2,1)S(1)} %get-tuple-element.18), channel_id=1, source_target_pairs={{1,0},{2,1},{3,2},{5,4},{6,5},{7,6},{9,8},{10,9},{11,10},{13,12},{... | collective-permute-start | bytes 147464 | tf_op jit(solution)/shard_map/ppermute | solution.py:16
  127.1 7.8 %collective-permute-start.9 = (bf16[192,1,128]{2,0,1:T(8,128)(2,1)S(1)}, bf16[192,1,128]{2,0,1:T(8,128)(2,1)S(1)}, u32[]{:S(2)}, u32[]{:S(2)}) collective-permute-start(bf16[192,1,128]{2,0,1:T(8,128)(2,1)S(1)} %get-tuple-element.17), channel_id=1, source_target_pairs={{0,1},{1,2},{2,3},{4,5},{5,6},{6,7},{8,9},{9,10},{10,11},{12,13},{... | collective-permute-start | bytes 147464 | tf_op jit(solution)/shard_map/ppermute | solution.py:13
  138.7 3.6 %collective-permute-start.11 = (bf16[72,16,128]{2,0,1:T(8,128)(2,1)S(1)}, bf16[72,16,128]{2,0,1:T(8,128)(2,1)S(1)}, u32[]{:S(2)}, u32[]{:S(2)}) collective-permute-start(bf16[72,16,128]{2,0,1:T(8,128)(2,1)S(1)} %fusion.104), channel_id=1, source_target_pairs={{4,0},{8,4},{12,8},{16,12},{20,16},{24,20},{28,24},{5,1},{9,5},{13... | collective-permute-start | bytes 884744 | tf_op jit(solution)/shard_map/ppermute | solution.py:24
  146.1 7.4 %collective-permute-start.13 = (bf16[72,4,128]{2,0,1:T(8,128)(2,1)S(1)}, bf16[72,4,128]{2,0,1:T(8,128)(2,1)S(1)}, u32[]{:S(2)}, u32[]{:S(2)}) collective-permute-start(bf16[72,4,128]{2,0,1:T(8,128)(2,1)S(1)} %get-tuple-element.21), channel_id=1, source_target_pairs={{1,0},{2,1},{3,2},{5,4},{6,5},{7,6},{9,8},{10,9},{11,10},{13,12},{... | collective-permute-start | bytes 221192 | tf_op jit(solution)/shard_map/ppermute | solution.py:16
  147.4 6.5 %collective-permute-start.12 = (bf16[72,4,128]{2,0,1:T(8,128)(2,1)S(1)}, bf16[72,4,128]{2,0,1:T(8,128)(2,1)S(1)}, u32[]{:S(2)}, u32[]{:S(2)}) collective-permute-start(bf16[72,4,128]{2,0,1:T(8,128)(2,1)S(1)} %get-tuple-element.22), channel_id=1, source_target_pairs={{0,1},{1,2},{2,3},{4,5},{5,6},{6,7},{8,9},{9,10},{10,11},{12,13},{... | collective-permute-start | bytes 221192 | tf_op jit(solution)/shard_map/ppermute | solution.py:13
  164.6 8.4 %collective-permute-start.15 = (bf16[192,2,128]{2,0,1:T(8,128)(2,1)S(1)}, bf16[192,2,128]{2,0,1:T(8,128)(2,1)S(1)}, u32[]{:S(2)}, u32[]{:S(2)}) collective-permute-start(bf16[192,2,128]{2,0,1:T(8,128)(2,1)S(1)} %get-tuple-element.15), channel_id=1, source_target_pairs={{1,0},{2,1},{3,2},{5,4},{6,5},{7,6},{9,8},{10,9},{11,10},{13,12},{... | collective-permute-start | bytes 294920 | tf_op jit(solution)/shard_map/ppermute | solution.py:16
  165.9 7.1 %collective-permute-start.14 = (bf16[192,2,128]{2,0,1:T(8,128)(2,1)S(1)}, bf16[192,2,128]{2,0,1:T(8,128)(2,1)S(1)}, u32[]{:S(2)}, u32[]{:S(2)}) collective-permute-start(bf16[192,2,128]{2,0,1:T(8,128)(2,1)S(1)} %get-tuple-element.16), channel_id=1, source_target_pairs={{0,1},{1,2},{2,3},{4,5},{5,6},{6,7},{8,9},{9,10},{10,11},{12,13},{... | collective-permute-start | bytes 294920 | tf_op jit(solution)/shard_map/ppermute | solution.py:13
  181.3 7.7 %copy-start.14 = (bf16[72,7,128]{2,0,1:T(8,128)(2,1)S(1)}, bf16[72,7,128]{2,0,1:T(8,128)(2,1)}, u32[]{:S(2)}) copy-start(bf16[72,7,128]{2,0,1:T(8,128)(2,1)} %copy-done.13) | copy-start | bytes 387076
  182.5 8.3 %collective-permute-start.17 = (bf16[192,1,128]{2,0,1:T(8,128)(2,1)S(1)}, bf16[192,1,128]{2,0,1:T(8,128)(2,1)S(1)}, u32[]{:S(2)}, u32[]{:S(2)}) collective-permute-start(bf16[192,1,128]{2,0,1:T(8,128)(2,1)S(1)} %get-tuple-element.14), channel_id=1, source_target_pairs={{1,0},{2,1},{3,2},{5,4},{6,5},{7,6},{9,8},{10,9},{11,10},{13,12},{... | collective-permute-start | bytes 147464 | tf_op jit(solution)/shard_map/ppermute | solution.py:16
  183.8 7.0 %collective-permute-start.16 = (bf16[192,1,128]{2,0,1:T(8,128)(2,1)S(1)}, bf16[192,1,128]{2,0,1:T(8,128)(2,1)S(1)}, u32[]{:S(2)}, u32[]{:S(2)}) collective-permute-start(bf16[192,1,128]{2,0,1:T(8,128)(2,1)S(1)} %get-tuple-element.13), channel_id=1, source_target_pairs={{0,1},{1,2},{2,3},{4,5},{5,6},{6,7},{8,9},{9,10},{10,11},{12,13},{... | collective-permute-start | bytes 147464 | tf_op jit(solution)/shard_map/ppermute | solution.py:13
  (25 other events, 71.5 us)
Sparse Core Ops, SparseCore 0:
  190.9 146.4 all-reduce.18
where the time goes:
time: 355 us; the launch traced here: 349 us
  waiting for transfers between devices  150 us (42%)
  matrix products  110 us (31%)
  starting transfers between devices  51 us (14%)
  between operations  15.7 us (4%)
  other arithmetic  12.5 us (4%)
  local copies, waits for them, and re-layouts  9.15 us (3%)
    psum x1, waiting for transfers between devices, body(): lax.psum((late_grads[0] + early_grads[0], late_grads[1] + early_grads[1],...  142 us
    dot_general x54, matrix products, convolve(): jnp.einsum(pattern, kernel[tap_index], window, preferred_element_type=jnp...  47.8 us
    dot_general x54, matrix products, convolve_back(): jnp.einsum(pattern, kernel[tap_index], window, preferred_element_type=jnp...  39.9 us
    ppermute x8, starting transfers between devices, padded_2(): lax.ppermute(lax.slice_in_dim(block, block.shape[dim] - width, None, axis...  37.7 us
    dot_general x54, matrix products, kernel_terms(): jnp.einsum(pattern, window, grad_out, preferred_element_type=jnp.float32)  22.5 us
    ppermute x8, starting transfers between devices, padded_2(): lax.ppermute(lax.slice_in_dim(block, 0, width, axis=dim), axis, backward)  10.3 us
    unnamed x64, local copies, waits for them, and re-layouts  7.89 us
  transfers between devices with their start and end apart: 19, of which 5 were waited for; matrix products, arithmetic and copies ran while one was open for 11% of the time, Pallas kernels for 0%

commit v1 on v0

--- a/solution.py
+++ b/solution.py
@@ -128,14 +128,13 @@
         jnp.bfloat16
     )
     state_adjoint, early_grads = backward(early_cot, early_saved)
-    grand_total = lax.psum(
-        (
-            late_grads[0] + early_grads[0],
-            late_grads[1] + early_grads[1],
-            late_grads[2] + early_grads[2],
-        ),
-        ("step", "lat"),
+    grand_total = (
+        late_grads[0] + early_grads[0],
+        late_grads[1] + early_grads[1],
+        late_grads[2] + early_grads[2],
     )
+    for mesh_axis in ("lat", "step"):
+        grand_total = lax.psum(grand_total, mesh_axis)
     cell_count = 2.0 * lax.axis_size("step") * total_rows * state_in.shape[3]
     grad_scale = 1.0 / math.sqrt(cell_count)
     return (

time: 355 us -> 395 us (1.11)
  waiting for transfers between devices: 150 us -> 190 us
    psum x1 -> x2, waiting for transfers between devices: 142 us -> 182 us  [body(): grand_total = lax.psum(grand_total, mesh_axis)]
    unnamed x64 -> x76, local copies, waits for them, and re-layouts: 7.89 us -> 8.41 us
  transfers between devices with their start and end apart: 19 -> 20, of which waited for: 5 -> 7; matrix products, arithmetic and copies ran while one was open for 11% -> 11% of each run, Pallas kernels for 0% -> 0%
where the time goes in v1:
time: 395 us; the launch traced here: 389 us
  waiting for transfers between devices  190 us (48%)
  matrix products  110 us (28%)
  starting transfers between devices  51 us (13%)
  between operations  15.8 us (4%)
  other arithmetic  12.5 us (3%)
  local copies, waits for them, and re-layouts  9.69 us (2%)
    psum x2, waiting for transfers between devices, body(): grand_total = lax.psum(grand_total, mesh_axis)  182 us
    dot_general x54, matrix products, convolve(): jnp.einsum(pattern, kernel[tap_index], window, preferred_element_type=jnp...  45.3 us
    dot_general x54, matrix products, convolve_back(): jnp.einsum(pattern, kernel[tap_index], window, preferred_element_type=jnp...  41.8 us
    ppermute x8, starting transfers between devices, padded_2(): lax.ppermute(lax.slice_in_dim(block, block.shape[dim] - width, None, axis...  37.7 us
    dot_general x54, matrix products, kernel_terms(): jnp.einsum(pattern, window, grad_out, preferred_element_type=jnp.float32)  22.5 us
    ppermute x8, starting transfers between devices, padded_2(): lax.ppermute(lax.slice_in_dim(block, 0, width, axis=dim), axis, backward)  10.3 us
    unnamed x76, local copies, waits for them, and re-layouts  8.41 us
  transfers between devices with their start and end apart: 20, of which 7 were waited for; matrix products, arithmetic and copies ran while one was open for 11% of the time, Pallas kernels for 0%

profile of v1, /device:TPU:0, one launch (start us, length us, event | category | flops | bytes accessed | tf_op | source)
XLA Modules:
  0.0 388.5 jit_solution(7350537511024041613)
XLA Ops:
  8.4 5.0 %collective-permute-start = (bf16[72,7,128]{2,0,1:T(8,128)(2,1)S(1)}, bf16[72,7,128]{2,0,1:T(8,128)(2,1)S(1)}, u32[]{:S(2)}, u32[]{:S(2)}) collective-permute-start(bf16[72,7,128]{2,0,1:T(8,128)(2,1)S(1)} %get-tuple-element.30), channel_id=1, source_target_pairs={{0,1},{1,2},{2,3},{4,5},{5,6},{6,7},{8,9},{9,10},{10,11},{12,13},{... | collective-permute-start | bytes 387080 | tf_op jit(solution)/shard_map/ppermute | solution.py:13
  15.7 4.5 %collective-permute-start.5 = (bf16[72,4,128]{2,0,1:T(8,128)(2,1)S(1)}, bf16[72,4,128]{2,0,1:T(8,128)(2,1)S(1)}, u32[]{:S(2)}, u32[]{:S(2)}) collective-permute-start(bf16[72,4,128]{2,0,1:T(8,128)(2,1)S(1)} %get-tuple-element.27), channel_id=1, source_target_pairs={{0,1},{1,2},{2,3},{4,5},{5,6},{6,7},{8,9},{9,10},{10,11},{12,13},{... | collective-permute-start | bytes 221192 | tf_op jit(solution)/shard_map/ppermute | solution.py:13
  23.2 3.3 collective-permute-done.6
  27.0 1.6 fusion.338
  30.2 1.6 fusion.342
  39.2 4.0 %fusion.75 = (bf16[192,28,128]{2,0,1:T(8,128)(2,1)S(1)}, f32[192,28,128]{2,0,1:T(8,128)}) fusion(pred[28]{0:T(512)(128)(4,1)S(1)} %compare_and_fusion, bf16[9,72,192]{2,1,0:T(8,128)(2,1)S(1)} %copy-done.15, bf16[72,30,128]{2,0,1:T(8,128)(2,1)S(1)} %pad_maximum_fusion, f32[28,128,192]{1,2,0:T(8,128)S(1)} %fusion.470, f32[28,128,192]{1,2,0:T(8,128)S(1)} %fusion.273, ...), kind=kOutput, calls=%fused_computation.167 | convolution fusion | flops 111476736 | bytes 26739200 | tf_op jit(solution)/shard_map/co,crw->orw/dot_general | solution.py:43
  47.6 3.3 fusion.129
  58.1 1.6 fusion.346
  59.8 3.5 collective-permute-start.3
  67.3 2.9 collective-permute-done.4
  76.6 4.4 %fusion.74 = (bf16[192,28,128]{2,0,1:T(8,128)(2,1)S(1)}, f32[192,28,128]{2,0,1:T(8,128)}) fusion(pred[28]{0:T(512)(128)(4,1)S(1)} %compare_and_fusion, bf16[9,72,192]{2,1,0:T(8,128)(2,1)} %param.11, bf16[72,30,128]{2,0,1:T(8,128)(2,1)S(1)} %pad_maximum_fusion.1, f32[28,128,192]{1,2,0:T(8,128)S(1)} %fusion.468, f32[28,128,192]{1,2,0:T(8,128)S(1)} %fusion.279, ...), kind=kOutput, calls=%fused_computation.166 | convolution fusion | flops 111476736 | bytes 26738716 | tf_op jit(solution)/shard_map/co,crw->orw/dot_general | solution.py:43
  85.5 2.1 fusion.128
  87.5 6.0 %fusion.43 = bf16[192,16,128]{2,0,1:T(8,128)(2,1)S(1)} fusion(f32[16,128,192]{1,2,0:T(8,128)} %fusion.309, f32[16,128,192]{1,2,0:T(8,128)} %fusion.338, f32[16,128,192]{1,2,0:T(8,128)} %fusion.340, f32[192,16,128]{2,0,1:T(8,128)S(1)} %copy-done.10, f32[192,24,128]{2,0,1:T(8,128)S(1)} %get-tuple-element.39, f32[16,128,192]{1,2,0:T(8,128)} %fusion.342, ...), kind=kOutput, calls=%fused_computation.121 | convolution fusion | flops 67633152 | bytes 15273984 | tf_op jit(solution)/shard_map/oc,orw->crw/dot_general | solution.py:57
  97.5 4.8 %collective-permute-start.7 = (bf16[192,2,128]{2,0,1:T(8,128)(2,1)S(1)}, bf16[192,2,128]{2,0,1:T(8,128)(2,1)S(1)}, u32[]{:S(2)}, u32[]{:S(2)}) collective-permute-start(bf16[192,2,128]{2,0,1:T(8,128)(2,1)S(1)} %get-tuple-element.23), channel_id=1, source_target_pairs={{0,1},{1,2},{2,3},{4,5},{5,6},{6,7},{8,9},{9,10},{10,11},{12,13},{... | collective-permute-start | bytes 294920 | tf_op jit(solution)/shard_map/ppermute | solution.py:13
  115.8 1.7 fusion.50
  119.1 5.0 %collective-permute-start.9 = (bf16[192,1,128]{2,0,1:T(8,128)(2,1)S(1)}, bf16[192,1,128]{2,0,1:T(8,128)(2,1)S(1)}, u32[]{:S(2)}, u32[]{:S(2)}) collective-permute-start(bf16[192,1,128]{2,0,1:T(8,128)(2,1)S(1)} %get-tuple-element.20), channel_id=1, source_target_pairs={{0,1},{1,2},{2,3},{4,5},{5,6},{6,7},{8,9},{9,10},{10,11},{12,13},{... | collective-permute-start | bytes 147464 | tf_op jit(solution)/shard_map/ppermute | solution.py:13
  139.5 4.7 %collective-permute-start.12 = (bf16[72,4,128]{2,0,1:T(8,128)(2,1)S(1)}, bf16[72,4,128]{2,0,1:T(8,128)(2,1)S(1)}, u32[]{:S(2)}, u32[]{:S(2)}) collective-permute-start(bf16[72,4,128]{2,0,1:T(8,128)(2,1)S(1)} %get-tuple-element.25), channel_id=1, source_target_pairs={{0,1},{1,2},{2,3},{4,5},{5,6},{6,7},{8,9},{9,10},{10,11},{12,13},{... | collective-permute-start | bytes 221192 | tf_op jit(solution)/shard_map/ppermute | solution.py:13
  150.4 1.7 fusion.57
  157.9 5.1 %collective-permute-start.14 = (bf16[192,2,128]{2,0,1:T(8,128)(2,1)S(1)}, bf16[192,2,128]{2,0,1:T(8,128)(2,1)S(1)}, u32[]{:S(2)}, u32[]{:S(2)}) collective-permute-start(bf16[192,2,128]{2,0,1:T(8,128)(2,1)S(1)} %get-tuple-element.19), channel_id=1, source_target_pairs={{0,1},{1,2},{2,3},{4,5},{5,6},{6,7},{8,9},{9,10},{10,11},{12,13},{... | collective-permute-start | bytes 294920 | tf_op jit(solution)/shard_map/ppermute | solution.py:13
  169.6 1.7 fusion.64
  182.8 5.2 %collective-permute-start.16 = (bf16[192,1,128]{2,0,1:T(8,128)(2,1)S(1)}, bf16[192,1,128]{2,0,1:T(8,128)(2,1)S(1)}, u32[]{:S(2)}, u32[]{:S(2)}) collective-permute-start(bf16[192,1,128]{2,0,1:T(8,128)(2,1)S(1)} %get-tuple-element.16), channel_id=1, source_target_pairs={{0,1},{1,2},{2,3},{4,5},{5,6},{6,7},{8,9},{9,10},{10,11},{12,13},{... | collective-permute-start | bytes 147464 | tf_op jit(solution)/shard_map/ppermute | solution.py:13
  191.9 113.4 %all-reduce.23.cloned.1.call-done = (f32[9,72,192]{2,1,0:T(8,128)}, f32[9,192,192]{2,1,0:T(8,128)}, f32[9,72,192]{2,1,0:T(8,128)}) async-done(((f32[9,72,192]{2,1,0:T(8,128)}, f32[9,192,192]{2,1,0:T(8,128)}, f32[9,72,192]{2,1,0:T(8,128)}), (f32[9,72,192]{2,1,0:T(8,128)}, f32[9,192,192]{2,1,0:T(8,128)}, f32[9,72,192]{2,1,0:T(8,128)})) %all-reduce.23.cloned.1.call-update) | async-done | bytes 2322448 | tf_op jit(solution)/shard_map/psum | solution.py:137
  309.2 68.2 %all-reduce.21.cloned.1.call-done = (f32[9,72,192]{2,1,0:T(8,128)}, f32[9,192,192]{2,1,0:T(8,128)}, f32[9,72,192]{2,1,0:T(8,128)}) async-done(((f32[9,72,192]{2,1,0:T(8,128)}, f32[9,192,192]{2,1,0:T(8,128)}, f32[9,72,192]{2,1,0:T(8,128)}), (f32[9,72,192]{2,1,0:T(8,128)}, f32[9,192,192]{2,1,0:T(8,128)}, f32[9,72,192]{2,1,0:T(8,128)})) %all-reduce.21.cloned.1.call-update) | async-done | bytes 2322448 | tf_op jit(solution)/shard_map/psum | solution.py:137
  377.3 2.9 broadcast_multiply_fusion
  (285 shorter events, 114.7 us)
Async XLA Ops:
  7.2 14.4 %copy-start = (bf16[1,72,16,128]{3,2,1,0:T(8,128)(2,1)S(1)}, bf16[1,72,16,128]{3,2,1,0:T(8,128)(2,1)}, u32[]{:S(2)}) copy-start(bf16[1,72,16,128]{3,2,1,0:T(8,128)(2,1)} %param.10) | copy-start | bytes 884740
  7.2 14.4 %copy-start.13 = (bf16[9,72,192]{2,1,0:T(8,128)(2,1)S(1)}, bf16[9,72,192]{2,1,0:T(8,128)(2,1)}, u32[]{:S(2)}) copy-start(bf16[9,72,192]{2,1,0:T(8,128)(2,1)} %param.13) | copy-start | bytes 746500
  7.2 298.1 %all-reduce.23.cloned.1.call-start = ((), (), s32[]{:S(2)}) async-start(), calls=%async_computation.1 | async-start | bytes 6193152 | tf_op jit(solution)/shard_map/psum | solution.py:137
  8.3 29.4 %copy-start.4 = (bf16[1,72,16,128]{3,1,2,0:T(8,128)(2,1)}, bf16[1,72,16,128]{3,1,2,0:T(8,128)(2,1)S(1)}, u32[]{:S(2)}) copy-start(bf16[1,72,16,128]{3,1,2,0:T(8,128)(2,1)S(1)} %copy.110) | copy-start | bytes 884740
  8.4 25.0 %collective-permute-start = (bf16[72,7,128]{2,0,1:T(8,128)(2,1)S(1)}, bf16[72,7,128]{2,0,1:T(8,128)(2,1)S(1)}, u32[]{:S(2)}, u32[]{:S(2)}) collective-permute-start(bf16[72,7,128]{2,0,1:T(8,128)(2,1)S(1)} %get-tuple-element.30), channel_id=1, source_target_pairs={{0,1},{1,2},{2,3},{4,5},{5,6},{6,7},{8,9},{9,10},{10,11},{12,13},{... | collective-permute-start | bytes 387080 | tf_op jit(solution)/shard_map/ppermute | solution.py:13
  13.3 20.0 %collective-permute-start.1 = (bf16[72,7,128]{2,0,1:T(8,128)(2,1)S(1)}, bf16[72,7,128]{2,0,1:T(8,128)(2,1)S(1)}, u32[]{:S(2)}, u32[]{:S(2)}) collective-permute-start(bf16[72,7,128]{2,0,1:T(8,128)(2,1)S(1)} %get-tuple-element.31), channel_id=1, source_target_pairs={{1,0},{2,1},{3,2},{5,4},{6,5},{7,6},{9,8},{10,9},{11,10},{13,12},{... | collective-permute-start | bytes 387080 | tf_op jit(solution)/shard_map/ppermute | solution.py:16
  15.7 7.5 %collective-permute-start.5 = (bf16[72,4,128]{2,0,1:T(8,128)(2,1)S(1)}, bf16[72,4,128]{2,0,1:T(8,128)(2,1)S(1)}, u32[]{:S(2)}, u32[]{:S(2)}) collective-permute-start(bf16[72,4,128]{2,0,1:T(8,128)(2,1)S(1)} %get-tuple-element.27), channel_id=1, source_target_pairs={{0,1},{1,2},{2,3},{4,5},{5,6},{6,7},{8,9},{9,10},{10,11},{12,13},{... | collective-permute-start | bytes 221192 | tf_op jit(solution)/shard_map/ppermute | solution.py:13
  20.3 6.2 %collective-permute-start.6 = (bf16[72,4,128]{2,0,1:T(8,128)(2,1)S(1)}, bf16[72,4,128]{2,0,1:T(8,128)(2,1)S(1)}, u32[]{:S(2)}, u32[]{:S(2)}) collective-permute-start(bf16[72,4,128]{2,0,1:T(8,128)(2,1)S(1)} %get-tuple-element.26), channel_id=1, source_target_pairs={{1,0},{2,1},{3,2},{5,4},{6,5},{7,6},{9,8},{10,9},{11,10},{13,12},{... | collective-permute-start | bytes 221192 | tf_op jit(solution)/shard_map/ppermute | solution.py:16
  27.0 31.1 %copy-start.6 = (bf16[72,24,136]{2,0,1:T(8,128)(2,1)}, bf16[72,24,136]{2,0,1:T(8,128)(2,1)S(1)}, u32[]{:S(2)}) copy-start(bf16[72,24,136]{2,0,1:T(8,128)(2,1)S(1)} %select_maximum_fusion.10) | copy-start | bytes 1410052
  55.1 4.6 %collective-permute-start.2 = (bf16[72,16,128]{2,0,1:T(8,128)(2,1)S(1)}, bf16[72,16,128]{2,0,1:T(8,128)(2,1)S(1)}, u32[]{:S(2)}, u32[]{:S(2)}) collective-permute-start(bf16[72,16,128]{2,0,1:T(8,128)(2,1)S(1)} %fusion.105), channel_id=1, source_target_pairs={{0,4},{4,8},{8,12},{12,16},{16,20},{20,24},{24,28},{1,5},{5,9},{9,... | collective-permute-start | bytes 884744 | tf_op jit(solution)/shard_map/ppermute | solution.py:24
  59.8 7.4 %collective-permute-start.3 = (bf16[72,7,128]{2,0,1:T(8,128)(2,1)S(1)}, bf16[72,7,128]{2,0,1:T(8,128)(2,1)S(1)}, u32[]{:S(2)}, u32[]{:S(2)}) collective-permute-start(bf16[72,7,128]{2,0,1:T(8,128)(2,1)S(1)} %get-tuple-element.28), channel_id=1, source_target_pairs={{0,1},{1,2},{2,3},{4,5},{5,6},{6,7},{8,9},{9,10},{10,11},{12,13},{... | collective-permute-start | bytes 387080 | tf_op jit(solution)/shard_map/ppermute | solution.py:13
  63.3 6.8 %collective-permute-start.4 = (bf16[72,7,128]{2,0,1:T(8,128)(2,1)S(1)}, bf16[72,7,128]{2,0,1:T(8,128)(2,1)S(1)}, u32[]{:S(2)}, u32[]{:S(2)}) collective-permute-start(bf16[72,7,128]{2,0,1:T(8,128)(2,1)S(1)} %get-tuple-element.29), channel_id=1, source_target_pairs={{1,0},{2,1},{3,2},{5,4},{6,5},{7,6},{9,8},{10,9},{11,10},{13,12},{... | collective-permute-start | bytes 387080 | tf_op jit(solution)/shard_map/ppermute | solution.py:16
  96.2 14.6 %collective-permute-start.8 = (bf16[192,2,128]{2,0,1:T(8,128)(2,1)S(1)}, bf16[192,2,128]{2,0,1:T(8,128)(2,1)S(1)}, u32[]{:S(2)}, u32[]{:S(2)}) collective-permute-start(bf16[192,2,128]{2,0,1:T(8,128)(2,1)S(1)} %get-tuple-element.22), channel_id=1, source_target_pairs={{1,0},{2,1},{3,2},{5,4},{6,5},{7,6},{9,8},{10,9},{11,10},{13,12},{... | collective-permute-start | bytes 294920 | tf_op jit(solution)/shard_map/ppermute | solution.py:16
  97.5 13.3 %collective-permute-start.7 = (bf16[192,2,128]{2,0,1:T(8,128)(2,1)S(1)}, bf16[192,2,128]{2,0,1:T(8,128)(2,1)S(1)}, u32[]{:S(2)}, u32[]{:S(2)}) collective-permute-start(bf16[192,2,128]{2,0,1:T(8,128)(2,1)S(1)} %get-tuple-element.23), channel_id=1, source_target_pairs={{0,1},{1,2},{2,3},{4,5},{5,6},{6,7},{8,9},{9,10},{10,11},{12,13},{... | collective-permute-start | bytes 294920 | tf_op jit(solution)/shard_map/ppermute | solution.py:13
  117.8 9.1 %collective-permute-start.10 = (bf16[192,1,128]{2,0,1:T(8,128)(2,1)S(1)}, bf16[192,1,128]{2,0,1:T(8,128)(2,1)S(1)}, u32[]{:S(2)}, u32[]{:S(2)}) collective-permute-start(bf16[192,1,128]{2,0,1:T(8,128)(2,1)S(1)} %get-tuple-element.21), channel_id=1, source_target_pairs={{1,0},{2,1},{3,2},{5,4},{6,5},{7,6},{9,8},{10,9},{11,10},{13,12},{... | collective-permute-start | bytes 147464 | tf_op jit(solution)/shard_map/ppermute | solution.py:16
  119.1 7.8 %collective-permute-start.9 = (bf16[192,1,128]{2,0,1:T(8,128)(2,1)S(1)}, bf16[192,1,128]{2,0,1:T(8,128)(2,1)S(1)}, u32[]{:S(2)}, u32[]{:S(2)}) collective-permute-start(bf16[192,1,128]{2,0,1:T(8,128)(2,1)S(1)} %get-tuple-element.20), channel_id=1, source_target_pairs={{0,1},{1,2},{2,3},{4,5},{5,6},{6,7},{8,9},{9,10},{10,11},{12,13},{... | collective-permute-start | bytes 147464 | tf_op jit(solution)/shard_map/ppermute | solution.py:13
  130.7 3.6 collective-permute-start.11
  138.2 7.4 %collective-permute-start.13 = (bf16[72,4,128]{2,0,1:T(8,128)(2,1)S(1)}, bf16[72,4,128]{2,0,1:T(8,128)(2,1)S(1)}, u32[]{:S(2)}, u32[]{:S(2)}) collective-permute-start(bf16[72,4,128]{2,0,1:T(8,128)(2,1)S(1)} %get-tuple-element.24), channel_id=1, source_target_pairs={{1,0},{2,1},{3,2},{5,4},{6,5},{7,6},{9,8},{10,9},{11,10},{13,12},{... | collective-permute-start | bytes 221192 | tf_op jit(solution)/shard_map/ppermute | solution.py:16
  139.5 6.5 %collective-permute-start.12 = (bf16[72,4,128]{2,0,1:T(8,128)(2,1)S(1)}, bf16[72,4,128]{2,0,1:T(8,128)(2,1)S(1)}, u32[]{:S(2)}, u32[]{:S(2)}) collective-permute-start(bf16[72,4,128]{2,0,1:T(8,128)(2,1)S(1)} %get-tuple-element.25), channel_id=1, source_target_pairs={{0,1},{1,2},{2,3},{4,5},{5,6},{6,7},{8,9},{9,10},{10,11},{12,13},{... | collective-permute-start | bytes 221192 | tf_op jit(solution)/shard_map/ppermute | solution.py:13
  156.6 8.4 %collective-permute-start.15 = (bf16[192,2,128]{2,0,1:T(8,128)(2,1)S(1)}, bf16[192,2,128]{2,0,1:T(8,128)(2,1)S(1)}, u32[]{:S(2)}, u32[]{:S(2)}) collective-permute-start(bf16[192,2,128]{2,0,1:T(8,128)(2,1)S(1)} %get-tuple-element.18), channel_id=1, source_target_pairs={{1,0},{2,1},{3,2},{5,4},{6,5},{7,6},{9,8},{10,9},{11,10},{13,12},{... | collective-permute-start | bytes 294920 | tf_op jit(solution)/shard_map/ppermute | solution.py:16
  157.9 7.1 %collective-permute-start.14 = (bf16[192,2,128]{2,0,1:T(8,128)(2,1)S(1)}, bf16[192,2,128]{2,0,1:T(8,128)(2,1)S(1)}, u32[]{:S(2)}, u32[]{:S(2)}) collective-permute-start(bf16[192,2,128]{2,0,1:T(8,128)(2,1)S(1)} %get-tuple-element.19), channel_id=1, source_target_pairs={{0,1},{1,2},{2,3},{4,5},{5,6},{6,7},{8,9},{9,10},{10,11},{12,13},{... | collective-permute-start | bytes 294920 | tf_op jit(solution)/shard_map/ppermute | solution.py:13
  175.8 201.5 %all-reduce.21.cloned.1.call-start = ((), (), s32[]{:S(2)}) async-start(), calls=%async_computation | async-start | bytes 6193152 | tf_op jit(solution)/shard_map/psum | solution.py:137
  181.2 6.8 %collective-permute-start.17 = (bf16[192,1,128]{2,0,1:T(8,128)(2,1)S(1)}, bf16[192,1,128]{2,0,1:T(8,128)(2,1)S(1)}, u32[]{:S(2)}, u32[]{:S(2)}) collective-permute-start(bf16[192,1,128]{2,0,1:T(8,128)(2,1)S(1)} %get-tuple-element.17), channel_id=1, source_target_pairs={{1,0},{2,1},{3,2},{5,4},{6,5},{7,6},{9,8},{10,9},{11,10},{13,12},{... | collective-permute-start | bytes 147464 | tf_op jit(solution)/shard_map/ppermute | solution.py:16
  182.8 6.7 %collective-permute-start.16 = (bf16[192,1,128]{2,0,1:T(8,128)(2,1)S(1)}, bf16[192,1,128]{2,0,1:T(8,128)(2,1)S(1)}, u32[]{:S(2)}, u32[]{:S(2)}) collective-permute-start(bf16[192,1,128]{2,0,1:T(8,128)(2,1)S(1)} %get-tuple-element.16), channel_id=1, source_target_pairs={{0,1},{1,2},{2,3},{4,5},{5,6},{6,7},{8,9},{9,10},{10,11},{12,13},{... | collective-permute-start | bytes 147464 | tf_op jit(solution)/shard_map/ppermute | solution.py:13
  (32 other events, 95.5 us)
Sparse Core Ops, SparseCore 0:
  176.0 129.2 all-reduce.22
  308.9 68.3 all-reduce.20
